TPU v7x, 512 devices: a whole 4x8x8 slice. The times are simulated.
512 devices in a mesh: pair: 64 (over z, x, core), slab: 8 (over y).
Axes of the slice: x: 4, y: 8, z: 8, core: 2. Of those that a mesh axis runs over, the one named last changes fastest.
Arguments:
- amps: bfloat16 [1024, 1024, 128], P(('pair', 'slab')), may hold values from -6 to 6
- symmetry: int32 [1024], replicated, may hold values from 0 to 3
- screen: int32 [64, 16, 16], P('pair'), may hold values 0 or 1
- owner: int32 [1024], replicated, may hold values from 0 to 63, as said below
- integrals: bfloat16 [64, 2048, 2048], P('pair', 'slab'), may hold values from -0.25 to 0.25
Outputs:
- residual: bfloat16 [1024, 64, 16, 128], P(('pair', 'slab'))
Inputs may be any that keep to these rules, and one draw needn't show every extreme that they name: Every owner from 0 to 63 holds exactly 16 tiles.
All inputs are finite; a program needn't handle non-finite values. No bound on the sum of `screen` on one device may be relied on, other than what follows from the above.
Results may differ from a plain program's by a relative error of at most 0.001.
Values may be sent and summed in bfloat16 or wider, within the bound.
A program may use at most 64 MiB of HBM per device.

v0:
```python
import jax
import jax.numpy as jnp
from jax import lax
from jax.sharding import PartitionSpec as P


def contract(operand, block_piece, mask_piece, per_owner, tile_width):
    rows_here = block_piece.shape[0]
    masked = (
        block_piece.reshape(rows_here, per_owner, tile_width) * mask_piece[:, :, None]
    ).reshape(rows_here, per_owner * tile_width)
    return jnp.dot(operand, masked, preferred_element_type=jnp.float32)


def on_device(amps, symmetry, screen, owner, integrals):
    n_pair = lax.axis_size("pair")
    local_rows, tile_count, tile_width = amps.shape
    per_owner = tile_count // n_pair
    owner_span = per_owner * tile_width
    tile_order = jnp.argsort(owner, stable=True).reshape(n_pair, per_owner)
    sorted_amps = jnp.take(amps, tile_order.reshape(-1), axis=1).reshape(
        local_rows, n_pair, owner_span
    )
    owned = lax.dynamic_index_in_dim(tile_order, lax.axis_index("pair"), 0, keepdims=False)
    labels = jnp.take(symmetry, owned)
    allowed = ((labels[:, None] == labels[None, :]) & (screen[0] == 1)).astype(jnp.bfloat16)
    mask_rows = jnp.repeat(allowed, tile_width, axis=0)
    block_rows = integrals[0]
    received = lax.all_to_all(sorted_amps, "pair", split_axis=1, concat_axis=1, tiled=True)
    flat_rows = received.reshape(local_rows * n_pair, owner_span)
    summed = contract(
        flat_rows,
        lax.all_gather(block_rows, "slab", axis=0, tiled=True),
        mask_rows,
        per_owner,
        tile_width,
    )
    product = summed.astype(jnp.bfloat16).reshape(local_rows, n_pair, owner_span)
    returned = lax.all_to_all(product, "pair", split_axis=1, concat_axis=1, tiled=True)
    return returned.reshape(local_rows, n_pair, per_owner, tile_width)


def solution(mesh):
    in_specs = (
        P(("pair", "slab"), None, None),
        P(),
        P("pair", None, None),
        P(),
        P("pair", "slab", None),
    )
    out_specs = P(("pair", "slab"), None, None, None)
    return jax.shard_map(
        on_device, mesh=mesh, in_specs=in_specs, out_specs=out_specs, check_vma=False
    )
```

profile of v0, /device:TPU:1, one launch (start us, length us, event | category | flops | bytes accessed | tf_op | source)
XLA Modules:
  0.0 163.3 jit_solution(9701086411608174818)
XLA Ops:
  6.5 0.0 copy-start
  6.5 0.0 copy-start.1
  6.5 0.0 copy-start.2
  6.5 0.0 all-gather.3.cloned.1.call-start
  6.5 0.7 all-gather.3.cloned.1.call-update
  7.3 5.1 %sort.17 = (s32[1024]{0:T(1024)}, s32[1024]{0:T(1024)S(1)}) sort(s32[1024]{0:T(1024)} %param.8, s32[1024]{0:T(1024)S(1)} %iota.4), dimensions={0}, to_apply=%region_0.0 | sort | flops 10240 | bytes 16384 | tf_op jit(solution)/shard_map/jit(argsort)/sort | solution.py:20
  12.3 0.1 broadcast_in_dim.25
  12.4 0.2 broadcast_in_dim.26
  12.6 0.1 copy.23
  12.7 0.0 copy-done
  12.7 4.4 %gather_fusion = bf16[1024,2,128]{2,0,1:T(8,128)(2,1)S(1)} fusion(bf16[2,1024,128]{2,1,0:T(8,128)(2,1)S(1)} %copy-done, s32[1024]{0:T(1024)S(1)} %fusion.5), kind=kCustom, calls=%fused_computation | custom fusion | bytes 1052672 | tf_op jit(solution)/shard_map/jit(_take)/gather | solution.py:21
  17.1 0.2 gather.13
  17.4 1.9 %broadcast_select_fusion = bf16[2,64,2048]{2,0,1:T(2,128)(2,1)} fusion(pred[64,2048]{1,0:T(8,128)(4,1)S(1)} %bitcast.43, bf16[2,64,2048]{2,1,0:T(8,128)(2,1)S(1)} %gather.13), kind=kLoop, calls=%fused_computation.7 | loop fusion | flops 262144 | bytes 1179648 | tf_op jit(solution)/shard_map/jit(_take)/select_n | solution.py:21
  19.2 14.8 %all-to-all-start = ((bf16[2,64,2048]{2,0,1:T(2,128)(2,1)}), bf16[2,64,2048]{2,0,1:T(2,128)(2,1)S(1)}, u32[]{:S(2)}, u32[]{:S(2)}) async-start(bf16[2,64,2048]{2,0,1:T(2,128)(2,1)} %broadcast_select_fusion), calls=%async_computation | async-start | bytes 1048576 | tf_op jit(solution)/shard_map/all_to_all | solution.py:29
  34.1 0.1 reshape.78
  34.2 0.0 copy-done.1
  34.2 0.6 gather_fusion.1
  34.9 0.0 copy-done.2
  34.9 0.1 fusion.4
  35.0 16.8 %all-to-all-done = bf16[2,64,2048]{2,0,1:T(2,128)(2,1)S(1)} async-done(((bf16[2,64,2048]{2,0,1:T(2,128)(2,1)}), bf16[2,64,2048]{2,0,1:T(2,128)(2,1)S(1)}, u32[]{:S(2)}, u32[]{:S(2)}) %all-to-all-start) | async-done | bytes 524320 | tf_op jit(solution)/shard_map/all_to_all | solution.py:29
  51.8 0.2 copy.10
  52.0 59.5 %all-gather.3.cloned.1.call-done = bf16[1,2048,2048]{2,1,0:T(8,128)(2,1)} async-done(((bf16[1,256,2048]{2,1,0:T(8,128)(2,1)}), bf16[1,2048,2048]{2,1,0:T(8,128)(2,1)}) %all-gather.3.cloned.1.call-update) | async-done | bytes 8388624 | tf_op jit(solution)/shard_map/all_gather | solution.py:33
  111.5 0.0 copy-start.3
  111.5 0.1 broadcast_in_dim.31
  111.5 9.0 %mul.14 = bf16[2048,16,128]{2,1,0:T(8,128)(2,1)S(1)} broadcast(bf16[2048,16]{1,0:T(8,128)(2,1)S(1)} %bitcast.41), dimensions={0,1} | broadcast | bytes 8454144 | tf_op jit(solution)/shard_map/mul | solution.py:10
  120.5 0.0 copy-done.3
  120.5 5.7 %fusion.3 = bf16[128,2048]{1,0:T(8,128)(2,1)S(1)} fusion(bf16[128,2048]{1,0:T(8,128)(2,1)S(1)} %bitcast.44, bf16[256,8,16,128]{3,2,1,0:T(8,128)(2,1)S(1)} %bitcast.40, bf16[1,2048,2048]{2,1,0:T(8,128)(2,1)S(1)} %copy-done.3), kind=kOutput, calls=%fused_computation.6 | convolution fusion | flops 1078198272 | bytes 17825792 | tf_op jit(solution)/shard_map/dot_general | solution.py:12
  126.2 0.5 copy.11
  126.7 28.5 %all_to_all.10 = bf16[2,64,2048]{2,0,1:T(2,128)(2,1)S(1)} all-to-all(bf16[2,64,2048]{2,0,1:T(2,128)(2,1)S(1)} %copy.11), channel_id=1, replica_groups=mesh['pair'=64,'slab'=8] {'pair'}, dimensions={1} | all-to-all | bytes 1048576 | tf_op jit(solution)/shard_map/all_to_all | solution.py:39
  155.3 0.3 reshape.80
  155.6 0.8 copy.12
  (7 shorter events, 0.1 us)
Async XLA Ops:
  6.5 6.2 %copy-start = (bf16[2,1024,128]{2,1,0:T(8,128)(2,1)S(1)}, bf16[2,1024,128]{2,1,0:T(8,128)(2,1)}, u32[]{:S(2)}) copy-start(bf16[2,1024,128]{2,1,0:T(8,128)(2,1)} %param.5) | copy-start | bytes 1572868
  6.5 27.7 %copy-start.1 = (s32[1024]{0:T(1024)S(1)}, s32[1024]{0:T(1024)}, u32[]{:S(2)}) copy-start(s32[1024]{0:T(1024)} %param.6) | copy-start | bytes 12292
  6.5 28.3 %copy-start.2 = (s32[1,16,16]{2,1,0:T(8,128)S(1)}, s32[1,16,16]{2,1,0:T(8,128)}, u32[]{:S(2)}) copy-start(s32[1,16,16]{2,1,0:T(8,128)} %param.7) | copy-start | bytes 3076
  6.5 104.9 %all-gather.3.cloned.1.call-start = ((), (), s32[]{:S(2)}) async-start(), calls=%async_computation.2 | async-start | bytes 9437184 | tf_op jit(solution)/shard_map/all_gather | solution.py:33
  19.2 32.6 %all-to-all-start = ((bf16[2,64,2048]{2,0,1:T(2,128)(2,1)}), bf16[2,64,2048]{2,0,1:T(2,128)(2,1)S(1)}, u32[]{:S(2)}, u32[]{:S(2)}) async-start(bf16[2,64,2048]{2,0,1:T(2,128)(2,1)} %broadcast_select_fusion), calls=%async_computation | async-start | bytes 1048576 | tf_op jit(solution)/shard_map/all_to_all | solution.py:29
  111.5 9.0 %copy-start.3 = (bf16[1,2048,2048]{2,1,0:T(8,128)(2,1)S(1)}, bf16[1,2048,2048]{2,1,0:T(8,128)(2,1)}, u32[]{:S(2)}) copy-start(bf16[1,2048,2048]{2,1,0:T(8,128)(2,1)} %all-gather.3.cloned.1.call-done) | copy-start | bytes 25165828
Sparse Core Ops, SparseCore 0:
  9.4 101.9 all-gather.2
where the time goes:
time: 164 us; the launch traced here: 163 us
  waiting for transfers between devices  77 us (47%)
  blocking collectives  28.5 us (17%)
  local copies, waits for them, and re-layouts  16.6 us (10%)
  starting transfers between devices  14.8 us (9%)
  between operations  13.6 us (8%)
  other arithmetic  7.06 us (4%)
  matrix products  5.67 us (3%)
    all_gather x1, waiting for transfers between devices, on_device(): lax.all_gather(block_rows, 'slab', axis=0, tiled=True)  59.5 us
    all_to_all x1, blocking collectives, on_device(): lax.all_to_all(product, 'pair', split_axis=1, concat_axis=1, tiled=True)  28.5 us
    all_to_all x1, waiting for transfers between devices, on_device(): lax.all_to_all(sorted_amps, 'pair', split_axis=1, concat_axis=1, tiled=True)  16.8 us
    all_to_all x1, starting transfers between devices, on_device(): lax.all_to_all(sorted_amps, 'pair', split_axis=1, concat_axis=1, tiled=True)  14.8 us
    mul x1, local copies, waits for them, and re-layouts, contract(): block_piece.reshape(rows_here, per_owner, tile_width)  8.96 us
    dot_general x1, matrix products, contract(): return jnp.dot(operand, masked, preferred_element_type=jnp.float32)  5.67 us
    sort x1, other arithmetic, on_device(): tile_order = jnp.argsort(owner, stable=True).reshape(n_pair, per_owner)  5.05 us
    gather x2, local copies, waits for them, and re-layouts, on_device(): jnp.take(amps, tile_order.reshape(-1), axis=1)  4.62 us
  transfers between devices with their start and end apart: 2, of which 2 were waited for; matrix products, arithmetic and copies ran while one was open for 8% of the time, Pallas kernels for 0%

commit v1 on v0

--- a/solution.py
+++ b/solution.py
@@ -28,13 +28,15 @@
     block_rows = integrals[0]
     received = lax.all_to_all(sorted_amps, "pair", split_axis=1, concat_axis=1, tiled=True)
     flat_rows = received.reshape(local_rows * n_pair, owner_span)
-    summed = contract(
-        flat_rows,
-        lax.all_gather(block_rows, "slab", axis=0, tiled=True),
-        mask_rows,
-        per_owner,
-        tile_width,
-    )
+
+    def orders_press(vec, on_dim):
+        val = jnp.concatenate(
+            lax.all_to_all(jnp.stack([vec for _ in range(lax.axis_size("slab"))]), "slab", 0, 0),
+            on_dim,
+        )
+        return val
+
+    summed = contract(flat_rows, orders_press(block_rows, 0), mask_rows, per_owner, tile_width)
     product = summed.astype(jnp.bfloat16).reshape(local_rows, n_pair, owner_span)
     returned = lax.all_to_all(product, "pair", split_axis=1, concat_axis=1, tiled=True)
     return returned.reshape(local_rows, n_pair, per_owner, tile_width)

time: 164 us -> 276 us (1.68)
  waiting for transfers between devices: 77 us -> 163 us
  blocking collectives: 28.5 us -> 55.3 us
  local copies, waits for them, and re-layouts: 16.6 us -> 35.2 us
  between operations: 13.6 us -> 0.14 us
  starting transfers between devices: 14.8 us -> 6.95 us
  other arithmetic: 7.06 us -> 13.9 us
  matrix products: 5.67 us -> 1.26 us
    all_to_all x1, waiting for transfers between devices: 16.8 us -> 163 us  [orders_press(): lax.all_to_all(jnp.stack([vec for _ in range(lax.axis_size('slab'))]), 's...]
    all_gather x1 -> x0, waiting for transfers between devices: 59.5 us -> none  [on_device(): lax.all_gather(block_rows, 'slab', axis=0, tiled=True)]
    all_to_all x0 -> x1, blocking collectives: none -> 32.4 us  [on_device(): lax.all_to_all(sorted_amps, 'pair', split_axis=1, concat_axis=1, tiled=True)]
    mul x1 -> x2, local copies, waits for them, and re-layouts: 8.96 us -> 23.2 us  [contract(): block_piece.reshape(rows_here, per_owner, tile_width)]
    all_to_all x1, starting transfers between devices: 14.8 us -> 6.95 us  [orders_press(): lax.all_to_all(jnp.stack([vec for _ in range(lax.axis_size('slab'))]), 's...]
    mul x0 -> x1, other arithmetic: none -> 7.52 us  [contract(): block_piece.reshape(rows_here, per_owner, tile_width)]
    all_to_all x1, blocking collectives: 28.5 us -> 23 us  [on_device(): lax.all_to_all(product, 'pair', split_axis=1, concat_axis=1, tiled=True)]
    dot_general x1, matrix products: 5.67 us -> 1.26 us  [contract(): return jnp.dot(operand, masked, preferred_element_type=jnp.float32)]
  transfers between devices with their start and end apart: 2 -> 1, of which waited for: 2 -> 1; matrix products, arithmetic and copies ran while one was open for 8% -> 9% of each run, Pallas kernels for 0% -> 0%
where the time goes in v1:
time: 276 us; the launch traced here: 275 us
  waiting for transfers between devices  163 us (59%)
  blocking collectives  55.3 us (20%)
  local copies, waits for them, and re-layouts  35.2 us (13%)
  other arithmetic  13.9 us (5%)
  starting transfers between devices  6.95 us (3%)
    all_to_all x1, waiting for transfers between devices, orders_press(): lax.all_to_all(jnp.stack([vec for _ in range(lax.axis_size('slab'))]), 's...  163 us
    all_to_all x1, blocking collectives, on_device(): lax.all_to_all(sorted_amps, 'pair', split_axis=1, concat_axis=1, tiled=True)  32.4 us
    mul x2, local copies, waits for them, and re-layouts, contract(): block_piece.reshape(rows_here, per_owner, tile_width)  23.2 us
    all_to_all x1, blocking collectives, on_device(): lax.all_to_all(product, 'pair', split_axis=1, concat_axis=1, tiled=True)  23 us
    mul x1, other arithmetic, contract(): block_piece.reshape(rows_here, per_owner, tile_width)  7.52 us
    all_to_all x1, starting transfers between devices, orders_press(): lax.all_to_all(jnp.stack([vec for _ in range(lax.axis_size('slab'))]), 's...  6.95 us
  transfers between devices with their start and end apart: 1, of which 1 were waited for; matrix products, arithmetic and copies ran while one was open for 9% of the time, Pallas kernels for 0%

profile of v1, /device:TPU:1, one launch (start us, length us, event | category | flops | bytes accessed | tf_op | source)
XLA Modules:
  0.0 275.4 jit_solution(8613421309607307584)
XLA Ops:
  0.0 0.0 copy-start
  0.0 0.0 copy-start.2
  0.0 5.2 %sort.17 = (s32[1024]{0:T(1024)}, s32[1024]{0:T(1024)S(1)}) sort(s32[1024]{0:T(1024)} %param.8, s32[1024]{0:T(1024)S(1)} %iota.4), dimensions={0}, to_apply=%region_0.0 | sort | flops 10240 | bytes 16384 | tf_op jit(solution)/shard_map/jit(argsort)/sort | solution.py:20
  5.2 0.0 copy-done
  5.2 4.4 %gather_fusion = bf16[1024,2,128]{2,0,1:T(8,128)(2,1)S(1)} fusion(bf16[2,1024,128]{2,1,0:T(8,128)(2,1)S(1)} %copy-done, s32[1024]{0:T(1024)S(1)} %fusion.1), kind=kCustom, calls=%fused_computation | custom fusion | bytes 1052672 | tf_op jit(solution)/shard_map/jit(_take)/gather | solution.py:21
  9.6 0.2 gather.13
  9.8 0.1 broadcast_in_dim.25
  9.9 0.2 broadcast_in_dim.26
  10.1 0.1 copy.16
  10.2 1.1 broadcast_select_fusion
  11.3 32.4 %all_to_all.15 = bf16[2,64,2048]{2,0,1:T(2,128)(2,1)S(1)} all-to-all(bf16[2,64,2048]{2,0,1:T(2,128)(2,1)S(1)} %broadcast_select_fusion), channel_id=1, replica_groups=mesh['pair'=64,'slab'=8] {'pair'}, dimensions={1} | all-to-all | bytes 1048576 | tf_op jit(solution)/shard_map/all_to_all | solution.py:29
  43.7 0.0 copy-done.2
  43.7 4.3 %stack.3 = bf16[8,256,2048]{2,1,0:T(8,128)(2,1)} broadcast(bf16[256,2048]{1,0:T(8,128)(2,1)S(1)} %bitcast.35), dimensions={1,2} | broadcast | bytes 9437184 | tf_op jit(solution)/shard_map/stack | solution.py:34
  47.9 0.0 copy-start.1
  47.9 0.0 copy-start.3
  47.9 7.0 %all-to-all-start.1 = ((bf16[8,256,2048]{2,1,0:T(8,128)(2,1)}), bf16[8,256,2048]{2,1,0:T(8,128)(2,1)}, u32[]{:S(2)}, u32[]{:S(2)}) async-start(bf16[8,256,2048]{2,1,0:T(8,128)(2,1)} %stack.3), calls=%async_computation.1 | async-start | bytes 16777216 | tf_op jit(solution)/shard_map/all_to_all | solution.py:34
  54.9 0.1 reshape.81
  55.0 0.0 copy-done.1
  55.0 0.6 gather_fusion.1
  55.7 0.0 copy-done.3
  55.7 0.1 fusion
  55.8 0.1 broadcast_in_dim.31
  55.8 9.9 %mul.17 = bf16[2048,16,128]{2,1,0:T(8,128)(2,1)} broadcast(bf16[2048,16]{1,0:T(8,128)(2,1)S(1)} %bitcast.33), dimensions={0,1} | broadcast | bytes 8454144 | tf_op jit(solution)/shard_map/mul | solution.py:10
  65.8 13.3 %mul.18 = bf16[8,256,2048]{2,1,0:T(8,128)(2,1)} reshape(bf16[2048,16,128]{2,1,0:T(8,128)(2,1)} %mul.17) | data formatting | bytes 16777216 | tf_op jit(solution)/shard_map/mul | solution.py:10
  79.1 0.2 copy.10
  79.3 162.7 %all-to-all-done.1 = bf16[8,256,2048]{2,1,0:T(8,128)(2,1)} async-done(((bf16[8,256,2048]{2,1,0:T(8,128)(2,1)}), bf16[8,256,2048]{2,1,0:T(8,128)(2,1)}, u32[]{:S(2)}, u32[]{:S(2)}) %all-to-all-start.1) | async-done | bytes 8388640 | tf_op jit(solution)/shard_map/all_to_all | solution.py:34
  242.0 7.5 %mul.19 = bf16[8,256,2048]{2,1,0:T(8,128)(2,1)S(1)} multiply(bf16[8,256,2048]{2,1,0:T(8,128)(2,1)} %all-to-all-done.1, bf16[8,256,2048]{2,1,0:T(8,128)(2,1)} %mul.18) | non-fusion elementwise | flops 4194304 | bytes 25165824 | tf_op jit(solution)/shard_map/mul | solution.py:10
  249.5 1.3 convolution_convert_fusion
  250.8 0.5 copy.11
  251.3 23.0 %all_to_all.16 = bf16[2,64,2048]{2,0,1:T(2,128)(2,1)S(1)} all-to-all(bf16[2,64,2048]{2,0,1:T(2,128)(2,1)S(1)} %copy.11), channel_id=1, replica_groups=mesh['pair'=64,'slab'=8] {'pair'}, dimensions={1} | all-to-all | bytes 1048576 | tf_op jit(solution)/shard_map/all_to_all | solution.py:41
  274.3 0.3 reshape.83
  274.6 0.8 copy.12
  (7 shorter events, 0.1 us)
Async XLA Ops:
  0.0 5.2 %copy-start = (bf16[2,1024,128]{2,1,0:T(8,128)(2,1)S(1)}, bf16[2,1024,128]{2,1,0:T(8,128)(2,1)}, u32[]{:S(2)}) copy-start(bf16[2,1024,128]{2,1,0:T(8,128)(2,1)} %param.5) | copy-start | bytes 1572868
  0.0 43.7 %copy-start.2 = (bf16[1,256,2048]{2,1,0:T(8,128)(2,1)S(1)}, bf16[1,256,2048]{2,1,0:T(8,128)(2,1)}, u32[]{:S(2)}) copy-start(bf16[1,256,2048]{2,1,0:T(8,128)(2,1)} %param.9) | copy-start | bytes 3145732
  47.9 7.1 %copy-start.1 = (s32[1024]{0:T(1024)S(1)}, s32[1024]{0:T(1024)}, u32[]{:S(2)}) copy-start(s32[1024]{0:T(1024)} %param.6) | copy-start | bytes 12292
  47.9 7.7 %copy-start.3 = (s32[1,16,16]{2,1,0:T(8,128)S(1)}, s32[1,16,16]{2,1,0:T(8,128)}, u32[]{:S(2)}) copy-start(s32[1,16,16]{2,1,0:T(8,128)} %param.7) | copy-start | bytes 3076
  47.9 194.0 %all-to-all-start.1 = ((bf16[8,256,2048]{2,1,0:T(8,128)(2,1)}), bf16[8,256,2048]{2,1,0:T(8,128)(2,1)}, u32[]{:S(2)}, u32[]{:S(2)}) async-start(bf16[8,256,2048]{2,1,0:T(8,128)(2,1)} %stack.3), calls=%async_computation.1 | async-start | bytes 16777216 | tf_op jit(solution)/shard_map/all_to_all | solution.py:34
